TPU v7x, 256 devices: a whole 4x4x8 slice. The times are simulated.
256 devices in a mesh: ctx: 8 (over z_hi, core), vocab: 32 (over x, y, z_lo).
Axes of the slice: x: 4, y: 4, z: 8 (z_hi: 4, z_lo: 2; z = z_hi * 2 + z_lo), core: 2. Of those that a mesh axis runs over, the one named last changes fastest.
Arguments:
- hidden: bfloat16 [512, 2, 7168], P('ctx', None, 'vocab'), may hold values from -30 to 30
- head: bfloat16 [7168, 65536], P('ctx', 'vocab'), may hold values from -0.15 to 0.15
- targets: int32 [512, 2], P('ctx'), may hold values from 0 to 65535
- loss_weight: float32 [512, 2], P('ctx'), may hold values from 16 to 256
Outputs:
- token_loss: float32 [512, 2], P('ctx')
- grad_hidden: bfloat16 [512, 2, 7168], P('ctx', None, 'vocab')
All inputs are finite; a program needn't handle non-finite values.
Results may differ from a plain program's by a relative error of at most 0.0046.
Values may be sent and summed in bfloat16 or wider, within the bound.
A program may use at most 64 MiB of HBM per device.

v0:
```python
import jax
import jax.numpy as jnp
from jax import lax
from jax.sharding import PartitionSpec as P


def sent_to_all(x, axis):
    copies = jnp.broadcast_to(x, (lax.axis_size(axis), *x.shape))
    return lax.all_to_all(copies, axis, split_axis=0, concat_axis=0, tiled=True)


def gathered_once(x, axis):
    leaves = jax.tree.leaves(x)
    order = sorted(range(len(leaves)), key=lambda k: -leaves[k].size)
    width = (1, *leaves[order[0]].shape)[-1]
    lines = [
        jnp.pad(leaves[k].reshape(-1), (0, -leaves[k].size % width)).reshape(-1, width)
        for k in order
    ]
    both, at, found = (sent_to_all(jnp.concatenate(lines), axis), 0, {})
    for k, line in zip(order, lines):
        slab = both[:, at : at + len(line)].reshape(len(both), -1)
        found[k] = slab[:, : leaves[k].size].reshape(-1, *leaves[k].shape)
        at += len(line)
    numbers = iter(range(len(leaves)))
    return jax.tree.map(lambda _: found[next(numbers)], x)


def combined_pairwise(pieces, combine):
    while len(jax.tree.leaves(pieces)[0]) > 1:
        pieces = jax.vmap(combine)(
            *(jax.tree.map(lambda part: part[side::2], pieces) for side in (0, 1))
        )
    return jax.tree.map(lambda part: part[0], pieces)


def joined_all(x, axis, combine):
    pieces = gathered_once(x, axis)
    return combined_pairwise(pieces, combine)


def cut_along(x, dim, size):
    lengths = x.shape
    pieces = x.reshape(*lengths[:dim], size, lengths[dim] // size, *lengths[dim + 1 :])
    return jnp.moveaxis(pieces, dim, 0)


def summed_on_arrival(x, axis, dim):
    pieces = cut_along(x, dim, lax.axis_size(axis))
    arrived = lax.all_to_all(pieces, axis, split_axis=0, concat_axis=0, tiled=True)
    return arrived.sum(axis=0)


def combine_stats(first, second):
    first_max, first_sum, first_target = first
    second_max, second_sum, second_target = second
    joined = jnp.maximum(first_max, second_max)
    total = first_sum * jnp.exp(first_max - joined) + second_sum * jnp.exp(second_max - joined)
    return (joined, total, first_target + second_target)


def body(hidden, head, targets, loss_weight):
    group_rows = hidden.shape[0]
    depth_count = hidden.shape[1]
    flat_count = group_rows * depth_count
    ctx_count = lax.axis_size("ctx")
    vocab_count = lax.axis_size("vocab")
    vocab_index = lax.axis_index("vocab")
    vocab_local = head.shape[1]
    flat_hidden = hidden.reshape(flat_count, hidden.shape[2])
    flat_targets = targets.reshape(flat_count)
    flat_weights = loss_weight.reshape(flat_count)
    whole_width = lax.all_gather(flat_hidden, "vocab", axis=1, tiled=True)
    width_slab = lax.all_to_all(whole_width, "ctx", split_axis=1, concat_axis=0, tiled=True)
    logits = lax.psum_scatter(
        jnp.dot(width_slab, head, preferred_element_type=jnp.float32),
        "ctx",
        scatter_dimension=0,
        tiled=True,
    )
    columns = vocab_index * vocab_local + lax.broadcasted_iota(jnp.int32, logits.shape, 1)
    target_hit = columns == flat_targets[:, None]
    local_max = jnp.max(logits, axis=1)
    local_target = jnp.sum(jnp.where(target_hit, logits, 0.0), axis=1)
    local_sum = jnp.sum(jnp.exp(logits - local_max[:, None]), axis=1)
    row_max, sum_exp, target_logit = joined_all(
        (local_max, local_sum, local_target), "vocab", combine_stats
    )
    flat_loss = jnp.log(sum_exp) + row_max - target_logit
    token_loss = flat_loss.reshape(group_rows, depth_count)
    probabilities = jnp.exp(logits - row_max[:, None]) / sum_exp[:, None]
    dlogits = (flat_weights[:, None] * (probabilities - target_hit.astype(jnp.float32))).astype(
        jnp.bfloat16
    )
    grad_slab = lax.dot_general(
        lax.all_gather(dlogits, "ctx", axis=0, tiled=True),
        head,
        (((1,), (1,)), ((), ())),
        preferred_element_type=jnp.float32,
    )
    share_rows = flat_count // vocab_count
    slab_width = grad_slab.shape[1]
    blocks = grad_slab.reshape(ctx_count, vocab_count, share_rows, slab_width)
    reduced = summed_on_arrival(blocks, "vocab", 1).astype(jnp.bfloat16)
    landed = lax.all_to_all(
        lax.all_to_all(reduced, "ctx", split_axis=0, concat_axis=3, tiled=True),
        "vocab",
        split_axis=3,
        concat_axis=1,
        tiled=True,
    )
    grad_out = landed.reshape(group_rows, depth_count, landed.shape[3])
    return (token_loss, grad_out)


def solution(mesh):
    return jax.shard_map(
        body,
        mesh=mesh,
        in_specs=(P("ctx", None, "vocab"), P("ctx", "vocab"), P("ctx", None), P("ctx", None)),
        out_specs=(P("ctx", None), P("ctx", None, "vocab")),
        check_vma=False,
    )
```

profile of v0, /device:TPU:1, one launch (start us, length us, event | category | flops | bytes accessed | tf_op | source)
XLA Modules:
  0.0 565.0 jit_solution(5996300982655620662)
XLA Ops:
  8.9 141.3 %all-gather.3.cloned.1.call-done = bf16[128,7168]{0,1:T(8,128)(2,1)} async-done(((bf16[128,224]{0,1:T(8,128)(2,1)}), bf16[128,7168]{0,1:T(8,128)(2,1)}) %all-gather.3.cloned.1.call-update) | async-done | bytes 1835024 | tf_op jit(solution)/shard_map/all_gather | solution.py:73
  150.2 72.8 %all_to_all.62 = bf16[128,8,896]{0,2,1:T(8,128)(2,1)S(1)} all-to-all(bf16[128,8,896]{0,2,1:T(8,128)(2,1)} %bitcast.42), channel_id=1, replica_groups=mesh['ctx'=8,'vocab'=32] {'ctx'}, dimensions={1} | all-to-all | bytes 3670016 | tf_op jit(solution)/shard_map/all_to_all | solution.py:74
  222.9 2.7 copy.30
  225.6 10.3 %fusion.6 = f32[1024,2048]{1,0:T(8,128)} fusion(bf16[1024,896]{1,0:T(8,128)(2,1)} %bitcast.43, bf16[896,2048]{1,0:T(8,128)(2,1)} %param.5), kind=kOutput, calls=%fused_computation.20 | convolution fusion | flops 3758096384 | bytes 13893632 | tf_op jit(solution)/shard_map/dot_general | solution.py:76
  236.9 88.8 %reduce-scatter.2.cloned.1.call-done = f32[128,2048]{1,0:T(8,128)} async-done(((f32[1024,2048]{1,0:T(8,128)}), f32[128,2048]{1,0:T(8,128)}) %reduce-scatter.2.cloned.1.call-update) | async-done | bytes 1048592 | tf_op jit(solution)/shard_map/reduce_scatter | solution.py:75
  325.7 1.4 reduce_max.9
  327.0 1.6 exponential_reduce_fusion
  329.3 8.1 %all-to-all-start.1 = ((f32[32,3,128]{2,1,0:T(4,128)}), f32[32,3,128]{2,1,0:T(4,128)S(1)}, u32[]{:S(2)}, u32[]{:S(2)}) async-start(f32[32,3,128]{2,1,0:T(4,128)} %broadcast_in_dim.9), calls=%async_computation.2 | async-start | bytes 131072 | tf_op jit(solution)/shard_map/all_to_all | solution.py:9
  337.7 6.9 %all-to-all-done.1 = f32[32,3,128]{2,1,0:T(4,128)S(1)} async-done(((f32[32,3,128]{2,1,0:T(4,128)}), f32[32,3,128]{2,1,0:T(4,128)S(1)}, u32[]{:S(2)}, u32[]{:S(2)}) %all-to-all-start.1) | async-done | bytes 49184 | tf_op jit(solution)/shard_map/all_to_all | solution.py:9
  345.2 2.4 fusion.3
  347.7 51.8 %all-gather.5.cloned.1.call-done = bf16[1024,2048]{1,0:T(8,128)(2,1)} async-done(((bf16[128,2048]{1,0:T(8,128)(2,1)}), bf16[1024,2048]{1,0:T(8,128)(2,1)}) %all-gather.5.cloned.1.call-update) | async-done | bytes 4194320 | tf_op jit(solution)/shard_map/all_gather | solution.py:96
  399.5 9.7 %fusion.7 = f32[1024,896]{1,0:T(8,128)} fusion(bf16[1024,2048]{1,0:T(8,128)(2,1)} %all-gather.5.cloned.1.call-done, bf16[896,2048]{1,0:T(8,128)(2,1)} %param.5), kind=kOutput, calls=%fused_computation.21 | convolution fusion | flops 3758096384 | bytes 11534336 | tf_op jit(solution)/shard_map/dot_general | solution.py:95
  409.2 5.0 reshape_reshape.3
  414.2 3.1 copy.46
  417.2 52.6 %all_to_all.63 = f32[32,8,1,4,896]{4,3,1,2,0:T(4,128)} all-to-all(f32[32,8,1,4,896]{4,3,1,2,0:T(4,128)S(1)} %bitcast.38), channel_id=1, replica_groups=mesh['ctx'=8,'vocab'=32] {'vocab'}, dimensions={0} | all-to-all | bytes 7340032 | tf_op jit(solution)/shard_map/all_to_all | solution.py:50
  469.9 2.7 reduce_sum.29
  472.5 12.3 %all_to_all.64 = bf16[8,1,4,896]{3,2,1,0:T(4,128)(2,1)S(1)} all-to-all(bf16[8,1,4,896]{3,2,1,0:T(4,128)(2,1)S(1)} %bitcast.45), channel_id=1, replica_groups=mesh['ctx'=8,'vocab'=32] {'ctx'}, dimensions={0} | all-to-all | bytes 114688 | tf_op jit(solution)/shard_map/all_to_all | solution.py:106
  484.8 6.0 %copy.38 = bf16[1,1,4,7168]{2,1,0,3:T(2,128)(2,1)} copy(bf16[1,1,4,7168]{3,2,1,0:T(4,128)(2,1)S(1)} %bitcast.46) | data formatting | bytes 114688 | tf_op jit(solution)/shard_map/all_to_all | solution.py:106
  491.3 39.8 %reduce.5 = bf16[7168,4]{1,0:T(8,128)(2,1)S(1)} reduce(bf16[7168,1,1,4]{3,2,1,0:T(2,128)(2,1)} %bitcast.40, bf16[]{:T(256)} %broadcast.6), dimensions={1,2}, to_apply=%bitcast.31.reduce_sub_computation | reduce | bytes 114690
  531.1 2.5 reshape.69
  533.6 3.9 all-to-all-start.4
  538.2 6.5 %all-to-all-done.4 = bf16[32,2,448]{2,1,0:T(2,128)(2,1)S(1)} async-done(((bf16[32,2,448]{2,1,0:T(2,128)(2,1)}), bf16[32,2,448]{2,1,0:T(2,128)(2,1)S(1)}, u32[]{:S(2)}, u32[]{:S(2)}) %all-to-all-start.4) | async-done | bytes 57376 | tf_op jit(solution)/shard_map/all_to_all | solution.py:105
  544.7 5.7 %reshape.70 = bf16[7168,1,1,4]{3,2,1,0:T(2,128)(2,1)} reshape(bf16[32,2,448]{2,1,0:T(2,128)(2,1)S(1)} %all-to-all-done.4) | data formatting | bytes 114688
  550.5 7.1 %copy.39 = bf16[1,1,4,7168]{3,2,1,0:T(4,128)(2,1)S(1)} copy(bf16[1,1,4,7168]{2,1,0,3:T(2,128)(2,1)} %bitcast.39) | data formatting | bytes 114688 | tf_op jit(solution)/shard_map/all_to_all | solution.py:105
  (59 shorter events, 6.2 us)
Async XLA Ops:
  7.2 143.0 %all-gather.3.cloned.1.call-start = ((), (), s32[]{:S(2)}) async-start(), calls=%async_computation.6 | async-start | bytes 1892352 | tf_op jit(solution)/shard_map/all_gather | solution.py:73
  8.9 316.8 %reduce-scatter.2.cloned.1.call-start = ((), (), s32[]{:S(2)}) async-start(), calls=%async_computation.7 | async-start | bytes 9437184 | tf_op jit(solution)/shard_map/reduce_scatter | solution.py:75
  235.9 0.7 copy-start
  236.0 101.5 %copy-start.1 = (f32[64,2]{0,1:T(2,128)S(1)}, f32[64,2]{0,1:T(2,128)}, u32[]{:S(2)}) copy-start(f32[64,2]{0,1:T(2,128)} %param.7) | copy-start | bytes 1540
  329.3 15.3 %all-to-all-start.1 = ((f32[32,3,128]{2,1,0:T(4,128)}), f32[32,3,128]{2,1,0:T(4,128)S(1)}, u32[]{:S(2)}, u32[]{:S(2)}) async-start(f32[32,3,128]{2,1,0:T(4,128)} %broadcast_in_dim.9), calls=%async_computation.2 | async-start | bytes 131072 | tf_op jit(solution)/shard_map/all_to_all | solution.py:9
  337.4 62.1 %all-gather.5.cloned.1.call-start = ((), (), s32[]{:S(2)}) async-start(), calls=%async_computation.8 | async-start | bytes 4718592 | tf_op jit(solution)/shard_map/all_gather | solution.py:96
  533.6 11.1 %all-to-all-start.4 = ((bf16[32,2,448]{2,1,0:T(2,128)(2,1)}), bf16[32,2,448]{2,1,0:T(2,128)(2,1)S(1)}, u32[]{:S(2)}, u32[]{:S(2)}) async-start(bf16[32,2,448]{2,1,0:T(2,128)(2,1)} %reshape.69), calls=%async_computation.5 | async-start | bytes 131072 | tf_op jit(solution)/shard_map/all_to_all | solution.py:105
Sparse Core Ops, SparseCore 0:
  10.3 139.7 all-gather.2
  236.1 89.5 reduce-scatter.1
  347.8 51.6 all-gather.4
where the time goes:
time: 566 us; the launch traced here: 565 us
  waiting for transfers between devices  295 us (52%)
  blocking collectives  138 us (24%)
  other arithmetic  47.9 us (8%)
  local copies, waits for them, and re-layouts  38.1 us (7%)
  matrix products  20 us (4%)
  between operations  13.9 us (2%)
  starting transfers between devices  12.1 us (2%)
    all_gather x1, waiting for transfers between devices, body(): whole_width = lax.all_gather(flat_hidden, 'vocab', axis=1, tiled=True)  141 us
    reduce_scatter x1, waiting for transfers between devices, body(): lax.psum_scatter(jnp.dot(width_slab, head, preferred_element_type=jnp.flo...  88.8 us
    all_to_all x1, blocking collectives, body(): lax.all_to_all(whole_width, 'ctx', split_axis=1, concat_axis=0, tiled=True)  72.8 us
    all_to_all x1, blocking collectives, summed_on_arrival(): lax.all_to_all(pieces, axis, split_axis=0, concat_axis=0, tiled=True)  52.6 us
    all_gather x1, waiting for transfers between devices, body(): lax.all_gather(dlogits, 'ctx', axis=0, tiled=True)  51.8 us
    unnamed x1, other arithmetic  39.8 us
    all_to_all x1, blocking collectives, body(): lax.all_to_all(reduced, 'ctx', split_axis=0, concat_axis=3, tiled=True)  12.3 us
  transfers between devices with their start and end apart: 5, of which 5 were waited for; matrix products, arithmetic and copies ran while one was open for 0% of the time, Pallas kernels for 0%

commit v1 on v0

--- a/solution.py
+++ b/solution.py
@@ -102,12 +102,20 @@
     slab_width = grad_slab.shape[1]
     blocks = grad_slab.reshape(ctx_count, vocab_count, share_rows, slab_width)
     reduced = summed_on_arrival(blocks, "vocab", 1).astype(jnp.bfloat16)
-    landed = lax.all_to_all(
-        lax.all_to_all(reduced, "ctx", split_axis=0, concat_axis=3, tiled=True),
-        "vocab",
-        split_axis=3,
-        concat_axis=1,
-        tiled=True,
+    landed = jnp.concatenate(
+        lax.all_to_all(
+            jnp.stack(
+                jnp.split(
+                    lax.all_to_all(reduced, "ctx", split_axis=0, concat_axis=3, tiled=True),
+                    lax.axis_size("vocab"),
+                    axis=3,
+                )
+            ),
+            "vocab",
+            0,
+            0,
+        ),
+        axis=1,
     )
     grad_out = landed.reshape(group_rows, depth_count, landed.shape[3])
     return (token_loss, grad_out)

time: 566 us -> 524 us (0.926)
  other arithmetic: 47.9 us -> 8.19 us
    unnamed x1 -> x0, other arithmetic: 39.8 us -> none
    all_to_all x4 -> x0, local copies, waits for them, and re-layouts: 13.3 us -> none  [the longest x3 7.3 us: body(): lax.all_to_all(lax.all_to_all(reduced, 'ctx', split_axis=0, concat_axis=3...]
    unnamed x10 -> x38, local copies, waits for them, and re-layouts: 10.2 us -> 21.1 us
where the time goes in v1:
time: 524 us
  waiting for transfers between devices  295 us (56%)
  blocking collectives  138 us (26%)
  local copies, waits for them, and re-layouts  36.3 us (7%)
  matrix products  20 us (4%)
  between operations  13.9 us (3%)
  starting transfers between devices  12.2 us (2%)
  other arithmetic  8.19 us (2%)
    all_gather x1, waiting for transfers between devices, body(): whole_width = lax.all_gather(flat_hidden, 'vocab', axis=1, tiled=True)  141 us
    reduce_scatter x1, waiting for transfers between devices, body(): lax.psum_scatter(jnp.dot(width_slab, head, preferred_element_type=jnp.flo...  88.6 us
    all_to_all x1, blocking collectives, body(): lax.all_to_all(whole_width, 'ctx', split_axis=1, concat_axis=0, tiled=True)  72.8 us
    all_to_all x1, blocking collectives, summed_on_arrival(): lax.all_to_all(pieces, axis, split_axis=0, concat_axis=0, tiled=True)  52.6 us
    all_gather x1, waiting for transfers between devices, body(): lax.all_gather(dlogits, 'ctx', axis=0, tiled=True)  51.9 us
    unnamed x38, local copies, waits for them, and re-layouts  21.1 us
    all_to_all x1, blocking collectives, body(): lax.all_to_all(reduced, 'ctx', split_axis=0, concat_axis=3, tiled=True)  12.3 us
  transfers between devices with their start and end apart: 5, of which 5 were waited for; matrix products, arithmetic and copies ran while one was open for 0% of the time, Pallas kernels for 0%

profile of v1, /device:TPU:1, one launch (start us, length us, event | category | flops | bytes accessed | tf_op | source)
XLA Modules:
  0.0 523.6 jit_solution(2961222836083256144)
XLA Ops:
  7.2 0.9 reshape.50
  8.1 0.7 copy.84
  8.9 141.3 %all-gather.3.cloned.1.call-done = bf16[128,7168]{0,1:T(8,128)(2,1)} async-done(((bf16[128,224]{0,1:T(8,128)(2,1)}), bf16[128,7168]{0,1:T(8,128)(2,1)}) %all-gather.3.cloned.1.call-update) | async-done | bytes 1835024 | tf_op jit(solution)/shard_map/all_gather | solution.py:73
  150.2 72.8 %all_to_all.52 = bf16[128,8,896]{0,2,1:T(8,128)(2,1)S(1)} all-to-all(bf16[128,8,896]{0,2,1:T(8,128)(2,1)} %bitcast.163), channel_id=1, replica_groups=mesh['ctx'=8,'vocab'=32] {'ctx'}, dimensions={1} | all-to-all | bytes 3670016 | tf_op jit(solution)/shard_map/all_to_all | solution.py:74
  222.9 2.7 copy.85
  225.6 10.3 %fusion.6 = f32[1024,2048]{1,0:T(8,128)} fusion(bf16[1024,896]{1,0:T(8,128)(2,1)} %bitcast.164, bf16[896,2048]{1,0:T(8,128)(2,1)} %param.5), kind=kOutput, calls=%fused_computation.84 | convolution fusion | flops 3758096384 | bytes 13893632 | tf_op jit(solution)/shard_map/dot_general | solution.py:76
  236.8 88.6 %reduce-scatter.2.cloned.1.call-done = f32[128,2048]{1,0:T(8,128)} async-done(((f32[1024,2048]{1,0:T(8,128)}), f32[128,2048]{1,0:T(8,128)}) %reduce-scatter.2.cloned.1.call-update) | async-done | bytes 1048592 | tf_op jit(solution)/shard_map/reduce_scatter | solution.py:75
  325.5 1.4 reduce_max.9
  326.8 1.6 exponential_reduce_fusion
  329.1 8.3 %all-to-all-start.1 = ((f32[32,3,128]{2,1,0:T(4,128)}), f32[32,3,128]{2,1,0:T(4,128)S(1)}, u32[]{:S(2)}, u32[]{:S(2)}) async-start(f32[32,3,128]{2,1,0:T(4,128)} %broadcast_in_dim.9), calls=%async_computation.2 | async-start | bytes 131072 | tf_op jit(solution)/shard_map/all_to_all | solution.py:9
  337.7 6.9 %all-to-all-done.1 = f32[32,3,128]{2,1,0:T(4,128)S(1)} async-done(((f32[32,3,128]{2,1,0:T(4,128)}), f32[32,3,128]{2,1,0:T(4,128)S(1)}, u32[]{:S(2)}, u32[]{:S(2)}) %all-to-all-start.1) | async-done | bytes 49184 | tf_op jit(solution)/shard_map/all_to_all | solution.py:9
  345.2 2.4 fusion.3
  347.6 51.9 %all-gather.5.cloned.1.call-done = bf16[1024,2048]{1,0:T(8,128)(2,1)} async-done(((bf16[128,2048]{1,0:T(8,128)(2,1)}), bf16[1024,2048]{1,0:T(8,128)(2,1)}) %all-gather.5.cloned.1.call-update) | async-done | bytes 4194320 | tf_op jit(solution)/shard_map/all_gather | solution.py:96
  399.5 9.7 %fusion.7 = f32[1024,896]{1,0:T(8,128)} fusion(bf16[1024,2048]{1,0:T(8,128)(2,1)} %all-gather.5.cloned.1.call-done, bf16[896,2048]{1,0:T(8,128)(2,1)} %param.5), kind=kOutput, calls=%fused_computation.85 | convolution fusion | flops 3758096384 | bytes 11534336 | tf_op jit(solution)/shard_map/dot_general | solution.py:95
  409.2 5.0 reshape_reshape.6
  414.2 3.1 copy.98
  417.3 52.6 %all_to_all.53 = f32[32,8,1,4,896]{4,3,1,2,0:T(4,128)} all-to-all(f32[32,8,1,4,896]{4,3,1,2,0:T(4,128)S(1)} %bitcast.161), channel_id=1, replica_groups=mesh['ctx'=8,'vocab'=32] {'vocab'}, dimensions={0} | all-to-all | bytes 7340032 | tf_op jit(solution)/shard_map/all_to_all | solution.py:50
  469.9 2.7 reduce_sum.29
  472.6 12.3 %all_to_all.54 = bf16[8,1,4,896]{3,2,1,0:T(4,128)(2,1)S(1)} all-to-all(bf16[8,1,4,896]{3,2,1,0:T(4,128)(2,1)S(1)} %bitcast.197), channel_id=1, replica_groups=mesh['ctx'=8,'vocab'=32] {'ctx'}, dimensions={0} | all-to-all | bytes 114688 | tf_op jit(solution)/shard_map/all_to_all | solution.py:109
  485.5 0.7 constant_dynamic-update-slice_fusion.30
  486.1 0.7 constant_dynamic-update-slice_fusion.29
  505.2 3.9 all-to-all-start.4
  509.8 6.5 %all-to-all-done.4 = bf16[32,1,1,4,224]{4,3,2,1,0:T(4,128)(2,1)S(1)} async-done(((bf16[32,1,1,4,224]{4,3,2,1,0:T(4,128)(2,1)}), bf16[32,1,1,4,224]{4,3,2,1,0:T(4,128)(2,1)S(1)}, u32[]{:S(2)}, u32[]{:S(2)}) %all-to-all-start.4) | async-done | bytes 57376 | tf_op jit(solution)/shard_map/all_to_all | solution.py:106
  516.3 0.7 reshape_reshape.7
  (83 shorter events, 22.2 us)
Async XLA Ops:
  7.2 143.0 %all-gather.3.cloned.1.call-start = ((), (), s32[]{:S(2)}) async-start(), calls=%async_computation.6 | async-start | bytes 1892352 | tf_op jit(solution)/shard_map/all_gather | solution.py:73
  8.9 316.6 %reduce-scatter.2.cloned.1.call-start = ((), (), s32[]{:S(2)}) async-start(), calls=%async_computation.7 | async-start | bytes 9437184 | tf_op jit(solution)/shard_map/reduce_scatter | solution.py:75
  235.9 0.7 copy-start
  235.9 101.5 %copy-start.1 = (f32[64,2]{0,1:T(2,128)S(1)}, f32[64,2]{0,1:T(2,128)}, u32[]{:S(2)}) copy-start(f32[64,2]{0,1:T(2,128)} %param.7) | copy-start | bytes 1540
  329.1 15.5 %all-to-all-start.1 = ((f32[32,3,128]{2,1,0:T(4,128)}), f32[32,3,128]{2,1,0:T(4,128)S(1)}, u32[]{:S(2)}, u32[]{:S(2)}) async-start(f32[32,3,128]{2,1,0:T(4,128)} %broadcast_in_dim.9), calls=%async_computation.2 | async-start | bytes 131072 | tf_op jit(solution)/shard_map/all_to_all | solution.py:9
  337.4 62.1 %all-gather.5.cloned.1.call-start = ((), (), s32[]{:S(2)}) async-start(), calls=%async_computation.8 | async-start | bytes 4718592 | tf_op jit(solution)/shard_map/all_gather | solution.py:96
  505.2 11.1 %all-to-all-start.4 = ((bf16[32,1,1,4,224]{4,3,2,1,0:T(4,128)(2,1)}), bf16[32,1,1,4,224]{4,3,2,1,0:T(4,128)(2,1)S(1)}, u32[]{:S(2)}, u32[]{:S(2)}) async-start(bf16[32,1,1,4,224]{4,3,2,1,0:T(4,128)(2,1)} %constant_dynamic-update-slice_fusion), calls=%async_computation.5 | async-start | bytes 131072 | tf_op jit(solution)/shard_map/all_to_all | solution.py:106
Sparse Core Ops, SparseCore 0:
  10.3 139.7 all-gather.2
  236.1 89.3 reduce-scatter.1
  347.8 51.7 all-gather.4
